TPU v7x, 256 devices: a whole 4x4x8 slice. The times are simulated.
256 devices in a mesh: dp: 16 (over z, core), fsdp: 16 (over y, x).
Axes of the slice: x: 4, y: 4, z: 8, core: 2. Of those that a mesh axis runs over, the one named last changes fastest.
Arguments:
- hidden_in: bfloat16 [2048, 2304], P(('dp', 'fsdp')), may hold values from -30 to 30
- cache_pool: bfloat16 [8448, 16, 2, 2048], P('dp', None, None, 'fsdp'), may hold values from -64 to 64
- project_in: bfloat16 [2304, 3, 2048], P('dp', None, 'fsdp'), may hold values from -0.125 to 0.125
- project_out: bfloat16 [2048, 2304], P('fsdp', 'dp'), may hold values from -0.125 to 0.125
- norm_first: bfloat16 [2304], replicated, may hold values from 0.099609375 to 1.8984375
- norm_second: bfloat16 [2304], replicated, may hold values from 0.099609375 to 1.8984375
- router: bfloat16 [2304, 8], replicated, may hold values from -0.125 to 0.125
- gate_up: bfloat16 [8, 2304, 2, 5760], P(None, 'dp', None, 'fsdp'), may hold values from -0.125 to 0.125
- expert_down: bfloat16 [8, 2304, 5760], P(None, 'dp', 'fsdp'), may hold values from -0.078125 to 0.078125
- lengths: int32 [2048], replicated, may hold values from 65 to 128, as said below
- prompt_pages: int32 [64, 4], P('dp'), may hold values from 0 to 527, as said below
- own_pages: int32 [2048, 4], P('dp'), may hold values from 0 to 527, as said below
- groups: int32 [2048], P('dp'), may hold values from 0 to 3
- move_target: int32 [16, 8], replicated, may hold values from 0 to 15, as said below
- routes: int32 [2048, 2], P(('dp', 'fsdp')), may hold values from 0 to 7, all different within a row; in each aligned block of 8 rows (0 to 7, 8 to 15, ...) at most 4 rows name the same one
Outputs:
- layer_out: bfloat16 [2048, 2304], P(('dp', 'fsdp'))
Inputs may be any that keep to these rules, and one draw needn't show every extreme that they name: `lengths`: every request's cache holds its shared prompt's 4 * 16 positions and at least one more; some request holds 128. `prompt_pages`: within a row, the prompt pages of all its shared prompts and the own pages of all its requests are distinct pages. `own_pages`: within a row, the prompt pages of all its shared prompts and the own pages of all its requests are distinct pages. Row s sends its request slots 128 - 8 + j, j < 8, to rows move_target[s, j]; a row's 8 destinations are distinct and differ from s, and for each j every row is the destination of exactly one row. `routes`: in the 8 rows of one device no expert is named more than 4 times.
All inputs are finite; a program needn't handle non-finite values.
Results may differ from a plain program's by a relative error of at most 0.009.
Values may be sent and summed in bfloat16 or wider, within the bound.
A program may use at most 128 MiB of HBM per device.

v0:
```python
import jax
import jax.numpy as jnp
from jax import lax
from jax.sharding import PartitionSpec as P

HD = 64
CAP = 4


def rms_scale(values, scaling):
    return (
        values
        * lax.rsqrt(jnp.mean(values * values, axis=-1, keepdims=True) + 1e-06)
        * scaling.astype(jnp.float32)
    )


def rotate(tensor, position):
    half_dim = tensor.shape[-1] // 2
    channel = jnp.arange(half_dim, dtype=jnp.float32)
    inverse = jnp.exp(-jnp.log(10000.0) * 2.0 * channel / tensor.shape[-1])
    angles = position.astype(jnp.float32)[:, None, None] * inverse
    cosine = jnp.cos(angles)
    sine_part = jnp.sin(angles)
    first_half = tensor[..., :half_dim]
    second_half = tensor[..., half_dim:]
    return jnp.concatenate(
        [
            first_half * cosine - second_half * sine_part,
            second_half * cosine + first_half * sine_part,
        ],
        axis=-1,
    )


def local(
    hidden_in,
    cache_pool,
    project_in,
    project_out,
    norm_first,
    norm_second,
    router,
    gate_up,
    expert_down,
    lengths,
    prompt_pages,
    own_pages,
    groups,
    move_target,
    routes,
):
    rows_count = lax.axis_size("dp")
    fsdp_count = lax.axis_size("fsdp")
    my_row = lax.axis_index("dp")
    my_column = lax.axis_index("fsdp")
    req_local = hidden_in.shape[0]
    model_width = hidden_in.shape[1]
    req_row = req_local * fsdp_count
    movers = move_target.shape[1]
    staying = req_row - movers
    page_len = cache_pool.shape[1]
    head_cols = cache_pool.shape[3]
    heads_here = head_cols // HD
    span_total = (prompt_pages.shape[1] + own_pages.shape[1]) * page_len
    expert_count = router.shape[1]
    rows_per_expert = rows_count // expert_count
    slots_row = (CAP + rows_per_expert - 1) // rows_per_expert
    gate_send = jnp.repeat(gate_up, rows_per_expert, axis=0)
    down_send = jnp.repeat(expert_down, rows_per_expert, axis=0)
    row_tokens = lax.all_gather(hidden_in, "fsdp", axis=0, tiled=True)
    group_hit = (
        groups[:, None] == jnp.arange(prompt_pages.shape[0], dtype=jnp.int32)[None, :]
    ).astype(jnp.int32)
    prompt_list = jnp.sum(group_hit[:, :, None] * prompt_pages[None, :, :], axis=1)
    page_list = jnp.concatenate([prompt_list, own_pages], axis=1)
    mover_cache = cache_pool[page_list[staying:]]
    my_targets = move_target[my_row]
    send_select = (my_targets[:, None] == jnp.arange(rows_count, dtype=jnp.int32)[None, :]).astype(
        jnp.bfloat16
    )
    cache_send = jnp.einsum(
        "jd,jpqkc->dpqkc", send_select, mover_cache, preferred_element_type=jnp.float32
    ).astype(jnp.bfloat16)
    tokens_send = jnp.einsum(
        "jd,jc->dc", send_select, row_tokens[staying:], preferred_element_type=jnp.float32
    ).astype(jnp.bfloat16)
    cache_recv, tokens_recv = (
        lax.all_to_all(cache_send, "dp", split_axis=0, concat_axis=0, tiled=True),
        lax.all_to_all(tokens_send, "dp", split_axis=0, concat_axis=0, tiled=True),
    )
    arrive_hit = move_target == my_row
    arrive_select = arrive_hit.astype(jnp.bfloat16)
    arrived_cache = jnp.einsum(
        "sj,spqkc->jpqkc", arrive_select, cache_recv, preferred_element_type=jnp.float32
    ).astype(jnp.bfloat16)
    arrived_tokens = jnp.einsum(
        "sj,sc->jc", arrive_select, tokens_recv, preferred_element_type=jnp.float32
    ).astype(jnp.bfloat16)
    source_row = jnp.sum(
        arrive_hit.astype(jnp.int32) * jnp.arange(rows_count, dtype=jnp.int32)[:, None], axis=0
    )
    row_lengths = lax.dynamic_slice_in_dim(lengths, my_row * req_row, req_row)
    arrived_lengths = lengths[source_row * req_row + staying + jnp.arange(movers, dtype=jnp.int32)]
    position = jnp.concatenate([row_lengths[:staying], arrived_lengths])
    tokens_row = jnp.concatenate([row_tokens[:staying], arrived_tokens], axis=0)
    normed_attn = rms_scale(tokens_row.astype(jnp.float32), norm_first).astype(jnp.bfloat16)
    piece = lax.all_gather(project_in, "dp", axis=0, tiled=True)
    projected = jnp.dot(
        normed_attn,
        piece.reshape(piece.shape[0], 3 * head_cols),
        preferred_element_type=jnp.float32,
    )
    projected = projected.reshape(req_row, 3, heads_here, HD)
    query = rotate(projected[:, 0], position).astype(jnp.bfloat16)
    key_new = rotate(projected[:, 1], position).astype(jnp.bfloat16)
    value_new = projected[:, 2].astype(jnp.bfloat16)
    resident_cache = cache_pool[page_list[:staying]]
    cache_rows = jnp.concatenate([resident_cache, arrived_cache], axis=0).reshape(
        req_row, span_total, 2, heads_here, HD
    )
    key_rows = cache_rows[:, :, 0]
    value_rows = cache_rows[:, :, 1]
    scale_factor = HD ** (-0.5)
    scores = (
        jnp.einsum("nhd,nlhd->nhl", query, key_rows, preferred_element_type=jnp.float32)
        * scale_factor
    )
    valid_mask = jnp.arange(span_total, dtype=jnp.int32)[None, :] < position[:, None]
    scores = jnp.where(valid_mask[:, None, :], scores, -jnp.inf)
    own_score = (
        jnp.sum(query.astype(jnp.float32) * key_new.astype(jnp.float32), axis=-1) * scale_factor
    )
    highest = jnp.maximum(jnp.max(scores, axis=-1), own_score)
    weights_cache = jnp.exp(scores - highest[..., None])
    weight_own = jnp.exp(own_score - highest)
    denominator = jnp.sum(weights_cache, axis=-1) + weight_own
    probs_cache = (weights_cache / denominator[..., None]).astype(jnp.bfloat16)
    prob_own = (weight_own / denominator).astype(jnp.bfloat16)
    mixture = jnp.einsum(
        "nhl,nlhd->nhd", probs_cache, value_rows, preferred_element_type=jnp.float32
    )
    mixture = mixture + prob_own.astype(jnp.float32)[..., None] * value_new.astype(jnp.float32)
    heads_out = mixture.astype(jnp.bfloat16).reshape(req_row, head_cols)
    out_columns = lax.all_gather(project_out, "dp", axis=1, tiled=True)
    attn_proj = lax.psum_scatter(
        jnp.dot(heads_out, out_columns, preferred_element_type=jnp.float32),
        "fsdp",
        scatter_dimension=0,
        tiled=True,
    )
    mine_tokens = lax.dynamic_slice_in_dim(tokens_row, my_column * req_local, req_local, 0)
    resid = mine_tokens.astype(jnp.float32) + attn_proj
    moe_in = rms_scale(resid, norm_second).astype(jnp.bfloat16)
    logits = jnp.dot(moe_in, router, preferred_element_type=jnp.float32)
    expert_ids = jnp.arange(expert_count, dtype=jnp.int32)
    picked = routes[:, :, None] == expert_ids[None, None, :]
    chosen = jnp.sum(jnp.where(picked, logits[:, None, :], 0.0), axis=-1)
    weight_pair = jnp.stack(
        [jax.nn.sigmoid(chosen[:, 0] - chosen[:, 1]), jax.nn.sigmoid(chosen[:, 1] - chosen[:, 0])],
        axis=1,
    )
    mix_expert = jnp.sum(picked.astype(jnp.float32) * weight_pair[:, :, None], axis=1)
    member = jnp.sum(picked.astype(jnp.int32), axis=1)
    rank_expert = jnp.cumsum(member, axis=0) - member
    row_numbers = jnp.arange(rows_count, dtype=jnp.int32)
    expert_of_row = (row_numbers[:, None] // rows_per_expert == expert_ids[None, :]).astype(
        jnp.int32
    )
    replica_of_row = row_numbers % rows_per_expert
    member_row = jnp.sum(member[:, None, :] * expert_of_row[None, :, :], axis=-1)
    rank_row = jnp.sum(rank_expert[:, None, :] * expert_of_row[None, :, :], axis=-1)
    mix_row = jnp.sum(
        mix_expert[:, None, :] * expert_of_row[None, :, :].astype(jnp.float32), axis=-1
    )
    slot_ids = jnp.arange(slots_row, dtype=jnp.int32)
    wanted_rank = slot_ids[None, :, None] * rows_per_expert + replica_of_row[:, None, None]
    select = (member_row.T[:, None, :] == 1) & (rank_row.T[:, None, :] == wanted_rank)
    dispatch = jnp.einsum(
        "dst,tm->dsm", select.astype(jnp.bfloat16), moe_in, preferred_element_type=jnp.float32
    ).astype(jnp.bfloat16)
    received = lax.all_to_all(dispatch, "dp", split_axis=0, concat_axis=0, tiled=True)
    expert_tokens = lax.all_gather(received[None], "fsdp", axis=0, tiled=True)
    gate_whole, down_whole = (
        lax.all_to_all(gate_send, "dp", split_axis=0, concat_axis=1, tiled=True),
        lax.all_to_all(down_send, "dp", split_axis=0, concat_axis=1, tiled=True),
    )
    flattened = expert_tokens.reshape(-1, model_width)
    units_here = gate_up.shape[3]
    gate_cols = gate_whole[0].reshape(model_width, 2 * units_here)
    down_cols = down_whole[0]
    both_parts = jnp.dot(flattened, gate_cols, preferred_element_type=jnp.float32)
    activation = (jax.nn.silu(both_parts[:, :units_here]) * both_parts[:, units_here:]).astype(
        jnp.bfloat16
    )
    returned = lax.psum_scatter(
        lax.dot_general(
            activation, down_cols, (((1,), (1,)), ((), ())), preferred_element_type=jnp.float32
        ).astype(jnp.bfloat16),
        "fsdp",
        scatter_dimension=0,
        tiled=True,
    ).astype(jnp.float32)
    back_rows = lax.all_to_all(
        returned.reshape(rows_count, slots_row, model_width),
        "dp",
        split_axis=0,
        concat_axis=0,
        tiled=True,
    )
    coefficient = select.astype(jnp.float32) * mix_row.T[:, None, :]
    moe_total = jnp.einsum("dst,dsm->tm", coefficient, back_rows, precision=lax.Precision.HIGHEST)
    return (resid + moe_total).astype(jnp.bfloat16)


def solution(mesh):
    placed = (
        P(("dp", "fsdp"), None),
        P("dp", None, None, "fsdp"),
        P("dp", None, "fsdp"),
        P("fsdp", "dp"),
        P(),
        P(),
        P(),
        P(None, "dp", None, "fsdp"),
        P(None, "dp", "fsdp"),
        P(),
        P("dp", None),
        P("dp", None),
        P("dp"),
        P(),
        P(("dp", "fsdp"), None),
    )
    return jax.shard_map(
        local, mesh=mesh, in_specs=placed, out_specs=P(("dp", "fsdp"), None), check_vma=False
    )
```

profile of v0, /device:TPU:1, one launch (start us, length us, event | category | flops | bytes accessed | tf_op | source)
XLA Modules:
  0.0 533.4 jit_solution(7687817300184575141)
XLA Ops:
  7.3 20.2 %all_gather.12 = bf16[128,2304]{1,0:T(8,128)(2,1)S(1)} all-gather(bf16[8,2304]{1,0:T(8,128)(2,1)} %param.15), channel_id=1, replica_groups=mesh['dp'=16,'fsdp'=16] {'fsdp'}, dimensions={0}, use_global_device_ids=true | all-gather | bytes 626688 | tf_op jit(solution)/shard_map/all_gather | solution.py:71
  30.5 14.2 %all-to-all-start = ((bf16[16,2,1152]{2,1,0:T(2,128)(2,1)}), bf16[16,2,1152]{2,1,0:T(2,128)(2,1)S(1)}, u32[]{:S(2)}, u32[]{:S(2)}) async-start(bf16[16,2,1152]{2,1,0:T(2,128)(2,1)} %reshape.422), calls=%async_computation | async-start | bytes 147456 | tf_op jit(solution)/shard_map/all_to_all | solution.py:90
  53.7 27.4 %gather_fusion.1 = bf16[960,16,2,128]{3,2,1,0:T(2,128)(2,1)} fusion(bf16[528,16,2,128]{3,2,1,0:T(2,128)(2,1)} %param.16, s32[1024]{0:T(1024)S(1)} %pad_clamp_fusion.1), kind=kCustom, calls=%fused_computation.1 | custom fusion | bytes 15732480 | tf_op jit(solution)/shard_map/gather | solution.py:118
  81.0 7.4 %copy.105 = bf16[960,16,2,128]{3,1,2,0:T(8,128)(2,1)} copy(bf16[960,16,2,128]{3,2,1,0:T(2,128)(2,1)} %gather_fusion.1) | data formatting | bytes 15728640 | tf_op jit(solution)/shard_map/gather | solution.py:118
  88.4 7.4 %all-to-all-start.1 = ((bf16[16,8,16,2,128]{4,3,2,1,0:T(2,128)(2,1)}), bf16[16,8,16,2,128]{4,3,2,1,0:T(2,128)(2,1)S(1)}, u32[]{:S(2)}, u32[]{:S(2)}) async-start(bf16[16,8,16,2,128]{4,3,2,1,0:T(2,128)(2,1)} %copy.108), calls=%async_computation.1 | async-start | bytes 2097152 | tf_op jit(solution)/shard_map/all_to_all | solution.py:89
  97.1 37.6 %all_gather.14 = bf16[128,2304]{0,1:T(8,128)(2,1)S(1)} all-gather(bf16[128,144]{0,1:T(8,128)(2,1)S(1)} %copy-done.3), channel_id=1, replica_groups=mesh['dp'=16,'fsdp'=16] {'dp'}, dimensions={1}, use_global_device_ids=true | all-gather | bytes 626688 | tf_op jit(solution)/shard_map/all_gather | solution.py:145
  135.9 7.0 %pad_maximum_fusion = bf16[128,8,16,2,128]{4,2,3,1,0:T(8,128)(2,1)} fusion(bf16[8,8,16,2,128]{4,2,3,1,0:T(8,128)(2,1)S(1)} %copy.110, bf16[120,8,16,2,128]{4,2,3,1,0:T(8,128)(2,1)} %bitcast.84), kind=kLoop, calls=%fused_computation.3 | loop fusion | flops 4194304 | bytes 16777216 | tf_op jit(solution)/shard_map/concatenate | solution.py:119
  143.0 13.0 %copy.111 = bf16[128,8,16,2,128]{0,4,3,2,1:T(8,128)(2,1)} copy(bf16[128,8,16,2,128]{4,2,3,1,0:T(8,128)(2,1)} %pad_maximum_fusion) | data formatting | bytes 16777216 | tf_op jit(solution)/shard_map/concatenate | solution.py:119
  156.0 3.8 copy.103
  162.0 3.9 multiply_reduce_fusion.1
  173.1 91.7 %all-reduce.3.cloned.1.call-done = f32[128,2304]{1,0:T(8,128)} async-done(((f32[128,2304]{1,0:T(8,128)}), f32[128,2304]{1,0:T(8,128)}) %all-reduce.3.cloned.1.call-update) | async-done | bytes 1179664
  266.2 18.5 %all_to_all.45 = bf16[16,2,2304]{2,1,0:T(2,128)(2,1)} all-to-all(bf16[16,2,2304]{2,1,0:T(2,128)(2,1)S(1)} %copy.112), channel_id=1, replica_groups=mesh['dp'=16,'fsdp'=16] {'dp'}, dimensions={0} | all-to-all | bytes 294912 | tf_op jit(solution)/shard_map/all_to_all | solution.py:182
  284.7 5.1 broadcast_in_dim.37
  289.8 4.5 all-to-all-start.3
  295.1 78.4 %all-to-all-done.3 = bf16[16,144,2,360]{3,2,1,0:T(2,128)(2,1)} async-done(((bf16[16,144,2,360]{3,2,1,0:T(2,128)(2,1)}), bf16[16,144,2,360]{3,2,1,0:T(2,128)(2,1)}, u32[]{:S(2)}, u32[]{:S(2)}) %all-to-all-start.3) | async-done | bytes 3317792 | tf_op jit(solution)/shard_map/all_to_all | solution.py:185
  374.9 5.5 %all-to-all-start.4 = ((bf16[16,144,360]{2,1,0:T(8,128)(2,1)}), bf16[16,144,360]{2,1,0:T(8,128)(2,1)}, u32[]{:S(2)}, u32[]{:S(2)}) async-start(bf16[16,144,360]{2,1,0:T(8,128)(2,1)} %bitcast.30), calls=%async_computation.4 | async-start | bytes 3538944 | tf_op jit(solution)/shard_map/all_to_all | solution.py:186
  380.7 8.5 %reshape_squeeze.3 = bf16[2304,720]{1,0:T(8,128)(2,1)} reshape(bf16[16,144,2,360]{3,2,1,0:T(2,128)(2,1)} %all-to-all-done.3) | data formatting | bytes 6635520 | tf_op jit(solution)/shard_map/reshape;squeeze | solution.py:190
  389.2 4.9 reshape.373
  394.1 5.1 fusion.54
  399.2 23.7 %all-to-all-done.4 = bf16[16,144,360]{2,1,0:T(8,128)(2,1)} async-done(((bf16[16,144,360]{2,1,0:T(8,128)(2,1)}), bf16[16,144,360]{2,1,0:T(8,128)(2,1)}, u32[]{:S(2)}, u32[]{:S(2)}) %all-to-all-start.4) | async-done | bytes 1658912 | tf_op jit(solution)/shard_map/all_to_all | solution.py:186
  422.9 4.9 convolution_convert_fusion
  428.1 74.2 %reduce-scatter.2.cloned.1.call-done = bf16[32,2304]{1,0:T(8,128)(2,1)} async-done(((bf16[512,2304]{1,0:T(8,128)(2,1)}), bf16[32,2304]{1,0:T(8,128)(2,1)}) %reduce-scatter.2.cloned.1.call-update) | async-done | bytes 147472 | tf_op jit(solution)/shard_map/reduce_scatter | solution.py:196
  504.1 9.4 %all-to-all-start.5 = ((f32[16,2,2304]{2,1,0:T(2,128)}), f32[16,2,2304]{2,1,0:T(2,128)S(1)}, u32[]{:S(2)}, u32[]{:S(2)}) async-start(f32[16,2,2304]{2,1,0:T(2,128)} %reshape.380), calls=%async_computation.6 | async-start | bytes 589824 | tf_op jit(solution)/shard_map/all_to_all | solution.py:204
  513.7 12.2 %all-to-all-done.5 = f32[16,2,2304]{2,1,0:T(2,128)S(1)} async-done(((f32[16,2,2304]{2,1,0:T(2,128)}), f32[16,2,2304]{2,1,0:T(2,128)S(1)}, u32[]{:S(2)}, u32[]{:S(2)}) %all-to-all-start.5) | async-done | bytes 294944 | tf_op jit(solution)/shard_map/all_to_all | solution.py:204
  (106 shorter events, 30.7 us)
Async XLA Ops:
  6.5 421.2 %copy-start = (bf16[2304,8]{0,1:T(8,128)(2,1)S(1)}, bf16[2304,8]{0,1:T(8,128)(2,1)}, u32[]{:S(2)}) copy-start(bf16[2304,8]{0,1:T(8,128)(2,1)} %param.21) | copy-start | bytes 110596
  6.5 149.4 %all-gather.4.cloned.1.call-start = ((), (), s32[]{:S(2)}) async-start(), calls=%async_computation.7 | async-start | bytes 1880064 | tf_op jit(solution)/shard_map/all_gather | solution.py:108
  30.5 58.0 %all-to-all-start = ((bf16[16,2,1152]{2,1,0:T(2,128)(2,1)}), bf16[16,2,1152]{2,1,0:T(2,128)(2,1)S(1)}, u32[]{:S(2)}, u32[]{:S(2)}) async-start(bf16[16,2,1152]{2,1,0:T(2,128)(2,1)} %reshape.422), calls=%async_computation | async-start | bytes 147456 | tf_op jit(solution)/shard_map/all_to_all | solution.py:90
  81.0 7.4 %copy-start.6 = (bf16[2304]{0:T(1024)(128)(2,1)S(1)}, bf16[2304]{0:T(1024)(128)(2,1)}, u32[]{:S(2)}) copy-start(bf16[2304]{0:T(1024)(128)(2,1)} %param.19) | copy-start | bytes 13828
  81.0 14.8 %copy-start.4 = (s32[16,8]{0,1:T(8,128)S(1)}, s32[16,8]{0,1:T(8,128)}, u32[]{:S(2)}) copy-start(s32[16,8]{0,1:T(8,128)} %param.28) | copy-start | bytes 1540
  88.4 7.6 %copy-start.1 = (s32[2048]{0:T(1024)S(1)}, s32[2048]{0:T(1024)}, u32[]{:S(2)}) copy-start(s32[2048]{0:T(1024)} %param.24) | copy-start | bytes 24580
  88.4 8.6 %copy-start.3 = (bf16[128,144]{0,1:T(8,128)(2,1)S(1)}, bf16[128,144]{0,1:T(8,128)(2,1)}, u32[]{:S(2)}) copy-start(bf16[128,144]{0,1:T(8,128)(2,1)} %param.18) | copy-start | bytes 110596
  88.4 46.7 %all-to-all-start.1 = ((bf16[16,8,16,2,128]{4,3,2,1,0:T(2,128)(2,1)}), bf16[16,8,16,2,128]{4,3,2,1,0:T(2,128)(2,1)S(1)}, u32[]{:S(2)}, u32[]{:S(2)}) async-start(bf16[16,8,16,2,128]{4,3,2,1,0:T(2,128)(2,1)} %copy.108), calls=%async_computation.1 | async-start | bytes 2097152 | tf_op jit(solution)/shard_map/all_to_all | solution.py:89
  95.8 169.0 %all-reduce.3.cloned.1.call-start = ((), (), s32[]{:S(2)}) async-start(), calls=%async_computation.10 | async-start | bytes 2359296
  170.0 1.5 copy-start.5
  170.0 1.6 copy-start.7
  170.0 1.6 copy-start.8
  289.8 83.7 %copy-start.2 = (bf16[8,144,360]{2,1,0:T(8,128)(2,1)S(1)}, bf16[8,144,360]{2,1,0:T(8,128)(2,1)}, u32[]{:S(2)}) copy-start(bf16[8,144,360]{2,1,0:T(8,128)(2,1)} %param.23) | copy-start | bytes 2488324
  289.8 83.7 %all-to-all-start.3 = ((bf16[16,144,2,360]{3,2,1,0:T(2,128)(2,1)}), bf16[16,144,2,360]{3,2,1,0:T(2,128)(2,1)}, u32[]{:S(2)}, u32[]{:S(2)}) async-start(bf16[16,144,2,360]{3,2,1,0:T(2,128)(2,1)} %bitcast.85), calls=%async_computation.3 | async-start | bytes 7077888 | tf_op jit(solution)/shard_map/all_to_all | solution.py:185
  294.4 94.8 %all-gather.6.cloned.1.call-start = ((), (), s32[]{:S(2)}) async-start(), calls=%async_computation.9 | async-start | bytes 2506752 | tf_op jit(solution)/shard_map/all_gather | solution.py:183
  374.9 48.0 %all-to-all-start.4 = ((bf16[16,144,360]{2,1,0:T(8,128)(2,1)}), bf16[16,144,360]{2,1,0:T(8,128)(2,1)}, u32[]{:S(2)}, u32[]{:S(2)}) async-start(bf16[16,144,360]{2,1,0:T(8,128)(2,1)} %bitcast.30), calls=%async_computation.4 | async-start | bytes 3538944 | tf_op jit(solution)/shard_map/all_to_all | solution.py:186
  380.4 122.0 %reduce-scatter.2.cloned.1.call-start = ((), (), s32[]{:S(2)}) async-start(), calls=%async_computation.8 | async-start | bytes 2506752 | tf_op jit(solution)/shard_map/reduce_scatter | solution.py:196
  504.1 21.8 %all-to-all-start.5 = ((f32[16,2,2304]{2,1,0:T(2,128)}), f32[16,2,2304]{2,1,0:T(2,128)S(1)}, u32[]{:S(2)}, u32[]{:S(2)}) async-start(f32[16,2,2304]{2,1,0:T(2,128)} %reshape.380), calls=%async_computation.6 | async-start | bytes 589824 | tf_op jit(solution)/shard_map/all_to_all | solution.py:204
Sparse Core Ops, SparseCore 0:
  9.2 43.5 all-gather.3
  171.6 93.1 all-reduce.2
  297.6 48.1 all-gather.5
  427.9 74.4 reduce-scatter.1
where the time goes:
time: 535 us; the launch traced here: 533 us
  waiting for transfers between devices  282 us (53%)
  local copies, waits for them, and re-layouts  83.3 us (16%)
  blocking collectives  76.3 us (14%)
  starting transfers between devices  41.3 us (8%)
  other arithmetic  20 us (4%)
  matrix products  16.5 us (3%)
  between operations  14.2 us (3%)
    unnamed x5, waiting for transfers between devices  93.2 us
    all_to_all x1, waiting for transfers between devices, local(): lax.all_to_all(gate_send, 'dp', split_axis=0, concat_axis=1, tiled=True)  78.4 us
    reduce_scatter x1, waiting for transfers between devices, local(): lax.psum_scatter(lax.dot_general(activation, down_cols, (((1,), (1,)), ((...  74.2 us
    all_gather x1, blocking collectives, local(): out_columns = lax.all_gather(project_out, 'dp', axis=1, tiled=True)  37.6 us
    gather x2, local copies, waits for them, and re-layouts, local(): resident_cache = cache_pool[page_list[:staying]]  34.7 us
    all_to_all x1, waiting for transfers between devices, local(): lax.all_to_all(down_send, 'dp', split_axis=0, concat_axis=1, tiled=True)  23.7 us
    all_gather x1, blocking collectives, local(): row_tokens = lax.all_gather(hidden_in, 'fsdp', axis=0, tiled=True)  20.2 us
    all_to_all x1, blocking collectives, local(): lax.all_to_all(dispatch, 'dp', split_axis=0, concat_axis=0, tiled=True)  18.5 us
  transfers between devices with their start and end apart: 9, of which 5 were waited for; matrix products, arithmetic and copies ran while one was open for 17% of the time, Pallas kernels for 0%

commit v1 on v0

--- a/solution.py
+++ b/solution.py
@@ -68,7 +68,9 @@
     slots_row = (CAP + rows_per_expert - 1) // rows_per_expert
     gate_send = jnp.repeat(gate_up, rows_per_expert, axis=0)
     down_send = jnp.repeat(expert_down, rows_per_expert, axis=0)
-    row_tokens = lax.all_gather(hidden_in, "fsdp", axis=0, tiled=True)
+    row_tokens = jnp.concatenate(
+        lax.all_to_all(jnp.stack([hidden_in] * lax.axis_size("fsdp")), "fsdp", 0, 0), axis=0
+    )
     group_hit = (
         groups[:, None] == jnp.arange(prompt_pages.shape[0], dtype=jnp.int32)[None, :]
     ).astype(jnp.int32)

time: 535 us -> 507 us (0.948)
  blocking collectives: 76.3 us -> 37.3 us
  waiting for transfers between devices: 282 us -> 289 us
    all_gather x1 -> x0, blocking collectives: 20.2 us -> none  [local(): row_tokens = lax.all_gather(hidden_in, 'fsdp', axis=0, tiled=True)]
    all_gather x1, blocking collectives: 37.6 us -> 18.8 us  [local(): out_columns = lax.all_gather(project_out, 'dp', axis=1, tiled=True)]
    all_to_all x0 -> x1, starting transfers between devices: none -> 7.58 us  [local(): lax.all_to_all(jnp.stack([hidden_in] * lax.axis_size('fsdp')), 'fsdp', 0, 0)]
    all_to_all x1, waiting for transfers between devices: 0.01 us -> 6.32 us  [local(): lax.all_to_all(tokens_send, 'dp', split_axis=0, concat_axis=0, tiled=True)]
  transfers between devices with their start and end apart: 9 -> 10, of which waited for: 5 -> 7; matrix products, arithmetic and copies ran while one was open for 17% -> 19% of each run, Pallas kernels for 0% -> 0%
where the time goes in v1:
time: 507 us; the launch traced here: 505 us
  waiting for transfers between devices  289 us (57%)
  local copies, waits for them, and re-layouts  86.4 us (17%)
  starting transfers between devices  41.5 us (8%)
  blocking collectives  37.3 us (7%)
  other arithmetic  20.5 us (4%)
  matrix products  16.5 us (3%)
  between operations  14.1 us (3%)
    unnamed x5, waiting for transfers between devices  93.6 us
    all_to_all x1, waiting for transfers between devices, local(): lax.all_to_all(gate_send, 'dp', split_axis=0, concat_axis=1, tiled=True)  78.4 us
    reduce_scatter x1, waiting for transfers between devices, local(): lax.psum_scatter(lax.dot_general(activation, down_cols, (((1,), (1,)), ((...  74.2 us
    gather x2, local copies, waits for them, and re-layouts, local(): resident_cache = cache_pool[page_list[:staying]]  34.7 us
    all_to_all x1, waiting for transfers between devices, local(): lax.all_to_all(down_send, 'dp', split_axis=0, concat_axis=1, tiled=True)  23.7 us
    all_gather x1, blocking collectives, local(): out_columns = lax.all_gather(project_out, 'dp', axis=1, tiled=True)  18.8 us
    all_to_all x1, blocking collectives, local(): lax.all_to_all(dispatch, 'dp', split_axis=0, concat_axis=0, tiled=True)  18.5 us
    concatenate x1, local copies, waits for them, and re-layouts, local(): jnp.concatenate([resident_cache, arrived_cache], axis=0)  13 us
  transfers between devices with their start and end apart: 10, of which 7 were waited for; matrix products, arithmetic and copies ran while one was open for 19% of the time, Pallas kernels for 0%

profile of v1, /device:TPU:1, one launch (start us, length us, event | category | flops | bytes accessed | tf_op | source)
XLA Modules:
  0.0 505.0 jit_solution(11663005182843686577)
XLA Ops:
  8.9 7.6 %all-to-all-start = ((bf16[16,8,2304]{2,1,0:T(8,128)(2,1)}), bf16[16,8,2304]{2,1,0:T(8,128)(2,1)S(1)}, u32[]{:S(2)}, u32[]{:S(2)}) async-start(bf16[16,8,2304]{2,1,0:T(8,128)(2,1)} %stack.4), calls=%async_computation | async-start | bytes 1179648 | tf_op jit(solution)/shard_map/all_to_all | solution.py:72
  22.6 3.9 gather_fusion.2
  29.6 10.6 %all-to-all-start.1 = ((bf16[16,2,1152]{2,1,0:T(2,128)(2,1)}), bf16[16,2,1152]{2,1,0:T(2,128)(2,1)S(1)}, u32[]{:S(2)}, u32[]{:S(2)}) async-start(bf16[16,2,1152]{2,1,0:T(2,128)(2,1)} %reshape.427), calls=%async_computation.1 | async-start | bytes 147456 | tf_op jit(solution)/shard_map/all_to_all | solution.py:92
  42.5 6.3 %all-to-all-done.1 = bf16[16,2,1152]{2,1,0:T(2,128)(2,1)S(1)} async-done(((bf16[16,2,1152]{2,1,0:T(2,128)(2,1)}), bf16[16,2,1152]{2,1,0:T(2,128)(2,1)S(1)}, u32[]{:S(2)}, u32[]{:S(2)}) %all-to-all-start.1) | async-done | bytes 73760 | tf_op jit(solution)/shard_map/all_to_all | solution.py:92
  52.4 27.4 %gather_fusion.1 = bf16[960,16,2,128]{3,2,1,0:T(2,128)(2,1)} fusion(bf16[528,16,2,128]{3,2,1,0:T(2,128)(2,1)} %param.16, s32[1024]{0:T(1024)S(1)} %pad_clamp_fusion.1), kind=kCustom, calls=%fused_computation.1 | custom fusion | bytes 15732480 | tf_op jit(solution)/shard_map/gather | solution.py:120
  79.8 7.3 %copy.105 = bf16[960,16,2,128]{3,1,2,0:T(8,128)(2,1)} copy(bf16[960,16,2,128]{3,2,1,0:T(2,128)(2,1)} %gather_fusion.1) | data formatting | bytes 15728640 | tf_op jit(solution)/shard_map/gather | solution.py:120
  87.4 18.8 %all_gather.10 = bf16[128,2304]{0,1:T(8,128)(2,1)S(1)} all-gather(bf16[128,144]{0,1:T(8,128)(2,1)S(1)} %copy-done.2), channel_id=1, replica_groups=mesh['dp'=16,'fsdp'=16] {'dp'}, dimensions={1}, use_global_device_ids=true | all-gather | bytes 626688 | tf_op jit(solution)/shard_map/all_gather | solution.py:147
  107.5 7.0 %pad_maximum_fusion = bf16[128,8,16,2,128]{4,2,3,1,0:T(8,128)(2,1)} fusion(bf16[8,8,16,2,128]{4,2,3,1,0:T(8,128)(2,1)S(1)} %copy.110, bf16[120,8,16,2,128]{4,2,3,1,0:T(8,128)(2,1)} %bitcast.89), kind=kLoop, calls=%fused_computation.3 | loop fusion | flops 4194304 | bytes 16777216 | tf_op jit(solution)/shard_map/concatenate | solution.py:121
  114.5 13.0 %copy.111 = bf16[128,8,16,2,128]{0,4,3,2,1:T(8,128)(2,1)} copy(bf16[128,8,16,2,128]{4,2,3,1,0:T(8,128)(2,1)} %pad_maximum_fusion) | data formatting | bytes 16777216 | tf_op jit(solution)/shard_map/concatenate | solution.py:121
  133.6 3.9 multiply_reduce_fusion.1
  144.5 92.2 %all-reduce.3.cloned.1.call-done = f32[128,2304]{1,0:T(8,128)} async-done(((f32[128,2304]{1,0:T(8,128)}), f32[128,2304]{1,0:T(8,128)}) %all-reduce.3.cloned.1.call-update) | async-done | bytes 1179664
  238.0 18.5 %all_to_all.50 = bf16[16,2,2304]{2,1,0:T(2,128)(2,1)} all-to-all(bf16[16,2,2304]{2,1,0:T(2,128)(2,1)S(1)} %copy.112), channel_id=1, replica_groups=mesh['dp'=16,'fsdp'=16] {'dp'}, dimensions={0} | all-to-all | bytes 294912 | tf_op jit(solution)/shard_map/all_to_all | solution.py:184
  256.5 5.1 %broadcast_in_dim.37 = bf16[8,2,144,2,360]{4,3,2,1,0:T(2,128)(2,1)} broadcast(bf16[8,144,2,360]{3,2,1,0:T(2,128)(2,1)} %param.22), dimensions={0,2,3,4} | broadcast | bytes 4976640 | tf_op jit(solution)/shard_map/broadcast_in_dim | solution.py:69
  261.6 4.5 all-to-all-start.4
  266.9 78.4 %all-to-all-done.4 = bf16[16,144,2,360]{3,2,1,0:T(2,128)(2,1)} async-done(((bf16[16,144,2,360]{3,2,1,0:T(2,128)(2,1)}), bf16[16,144,2,360]{3,2,1,0:T(2,128)(2,1)}, u32[]{:S(2)}, u32[]{:S(2)}) %all-to-all-start.4) | async-done | bytes 3317792 | tf_op jit(solution)/shard_map/all_to_all | solution.py:187
  346.7 5.5 %all-to-all-start.5 = ((bf16[16,144,360]{2,1,0:T(8,128)(2,1)}), bf16[16,144,360]{2,1,0:T(8,128)(2,1)}, u32[]{:S(2)}, u32[]{:S(2)}) async-start(bf16[16,144,360]{2,1,0:T(8,128)(2,1)} %bitcast.32), calls=%async_computation.5 | async-start | bytes 3538944 | tf_op jit(solution)/shard_map/all_to_all | solution.py:188
  352.5 8.5 %reshape_squeeze.3 = bf16[2304,720]{1,0:T(8,128)(2,1)} reshape(bf16[16,144,2,360]{3,2,1,0:T(2,128)(2,1)} %all-to-all-done.4) | data formatting | bytes 6635520 | tf_op jit(solution)/shard_map/reshape;squeeze | solution.py:192
  361.0 4.9 reshape.378
  365.9 5.1 %fusion.53 = f32[512,720]{0,1:T(8,128)} fusion(bf16[512,2304]{1,0:T(8,128)(2,1)S(1)} %reshape.378, bf16[2304,720]{1,0:T(8,128)(2,1)} %reshape_squeeze.3), kind=kOutput, calls=%fused_computation.133 | convolution fusion | flops 1698693120 | bytes 7151616 | tf_op jit(solution)/shard_map/dot_general | solution.py:194
  371.0 23.7 %all-to-all-done.5 = bf16[16,144,360]{2,1,0:T(8,128)(2,1)} async-done(((bf16[16,144,360]{2,1,0:T(8,128)(2,1)}), bf16[16,144,360]{2,1,0:T(8,128)(2,1)}, u32[]{:S(2)}, u32[]{:S(2)}) %all-to-all-start.5) | async-done | bytes 1658912 | tf_op jit(solution)/shard_map/all_to_all | solution.py:188
  394.7 4.9 convolution_convert_fusion
  399.9 74.2 %reduce-scatter.2.cloned.1.call-done = bf16[32,2304]{1,0:T(8,128)(2,1)} async-done(((bf16[512,2304]{1,0:T(8,128)(2,1)}), bf16[32,2304]{1,0:T(8,128)(2,1)}) %reduce-scatter.2.cloned.1.call-update) | async-done | bytes 147472 | tf_op jit(solution)/shard_map/reduce_scatter | solution.py:198
  475.9 9.4 %all-to-all-start.6 = ((f32[16,2,2304]{2,1,0:T(2,128)}), f32[16,2,2304]{2,1,0:T(2,128)S(1)}, u32[]{:S(2)}, u32[]{:S(2)}) async-start(f32[16,2,2304]{2,1,0:T(2,128)} %reshape.385), calls=%async_computation.7 | async-start | bytes 589824 | tf_op jit(solution)/shard_map/all_to_all | solution.py:206
  485.4 12.2 %all-to-all-done.6 = f32[16,2,2304]{2,1,0:T(2,128)S(1)} async-done(((f32[16,2,2304]{2,1,0:T(2,128)}), f32[16,2,2304]{2,1,0:T(2,128)S(1)}, u32[]{:S(2)}, u32[]{:S(2)}) %all-to-all-start.6) | async-done | bytes 294944 | tf_op jit(solution)/shard_map/all_to_all | solution.py:206
  (104 shorter events, 38.1 us)
Async XLA Ops:
  6.5 393.0 %copy-start = (bf16[2304,8]{0,1:T(8,128)(2,1)S(1)}, bf16[2304,8]{0,1:T(8,128)(2,1)}, u32[]{:S(2)}) copy-start(bf16[2304,8]{0,1:T(8,128)(2,1)} %param.21) | copy-start | bytes 110596
  6.5 120.9 %all-gather.4.cloned.1.call-start = ((), (), s32[]{:S(2)}) async-start(), calls=%async_computation.8 | async-start | bytes 1880064 | tf_op jit(solution)/shard_map/all_gather | solution.py:110
  8.9 18.7 %all-to-all-start = ((bf16[16,8,2304]{2,1,0:T(8,128)(2,1)}), bf16[16,8,2304]{2,1,0:T(8,128)(2,1)S(1)}, u32[]{:S(2)}, u32[]{:S(2)}) async-start(bf16[16,8,2304]{2,1,0:T(8,128)(2,1)} %stack.4), calls=%async_computation | async-start | bytes 1179648 | tf_op jit(solution)/shard_map/all_to_all | solution.py:72
  29.6 19.1 %all-to-all-start.1 = ((bf16[16,2,1152]{2,1,0:T(2,128)(2,1)}), bf16[16,2,1152]{2,1,0:T(2,128)(2,1)S(1)}, u32[]{:S(2)}, u32[]{:S(2)}) async-start(bf16[16,2,1152]{2,1,0:T(2,128)(2,1)} %reshape.427), calls=%async_computation.1 | async-start | bytes 147456 | tf_op jit(solution)/shard_map/all_to_all | solution.py:92
  48.8 57.8 %all-to-all-start.2 = ((bf16[16,8,16,2,128]{4,3,2,1,0:T(2,128)(2,1)}), bf16[16,8,16,2,128]{4,3,2,1,0:T(2,128)(2,1)S(1)}, u32[]{:S(2)}, u32[]{:S(2)}) async-start(bf16[16,8,16,2,128]{4,3,2,1,0:T(2,128)(2,1)} %copy.108), calls=%async_computation.2 | async-start | bytes 2097152 | tf_op jit(solution)/shard_map/all_to_all | solution.py:91
  52.3 184.3 %all-reduce.3.cloned.1.call-start = ((), (), s32[]{:S(2)}) async-start(), calls=%async_computation.11 | async-start | bytes 2359296
  79.8 7.3 %copy-start.4 = (bf16[2304]{0:T(1024)(128)(2,1)S(1)}, bf16[2304]{0:T(1024)(128)(2,1)}, u32[]{:S(2)}) copy-start(bf16[2304]{0:T(1024)(128)(2,1)} %param.19) | copy-start | bytes 13828
  79.8 7.6 %copy-start.2 = (bf16[128,144]{0,1:T(8,128)(2,1)S(1)}, bf16[128,144]{0,1:T(8,128)(2,1)}, u32[]{:S(2)}) copy-start(bf16[128,144]{0,1:T(8,128)(2,1)} %param.18) | copy-start | bytes 110596
  141.4 1.5 copy-start.3
  141.4 1.6 copy-start.5
  141.4 1.6 copy-start.6
  261.6 83.7 %copy-start.1 = (bf16[8,144,360]{2,1,0:T(8,128)(2,1)S(1)}, bf16[8,144,360]{2,1,0:T(8,128)(2,1)}, u32[]{:S(2)}) copy-start(bf16[8,144,360]{2,1,0:T(8,128)(2,1)} %param.23) | copy-start | bytes 2488324
  261.6 83.7 %all-to-all-start.4 = ((bf16[16,144,2,360]{3,2,1,0:T(2,128)(2,1)}), bf16[16,144,2,360]{3,2,1,0:T(2,128)(2,1)}, u32[]{:S(2)}, u32[]{:S(2)}) async-start(bf16[16,144,2,360]{3,2,1,0:T(2,128)(2,1)} %bitcast.90), calls=%async_computation.4 | async-start | bytes 7077888 | tf_op jit(solution)/shard_map/all_to_all | solution.py:187
  266.2 94.8 %all-gather.6.cloned.1.call-start = ((), (), s32[]{:S(2)}) async-start(), calls=%async_computation.10 | async-start | bytes 2506752 | tf_op jit(solution)/shard_map/all_gather | solution.py:185
  346.7 48.0 %all-to-all-start.5 = ((bf16[16,144,360]{2,1,0:T(8,128)(2,1)}), bf16[16,144,360]{2,1,0:T(8,128)(2,1)}, u32[]{:S(2)}, u32[]{:S(2)}) async-start(bf16[16,144,360]{2,1,0:T(8,128)(2,1)} %bitcast.32), calls=%async_computation.5 | async-start | bytes 3538944 | tf_op jit(solution)/shard_map/all_to_all | solution.py:188
  352.2 121.9 %reduce-scatter.2.cloned.1.call-start = ((), (), s32[]{:S(2)}) async-start(), calls=%async_computation.9 | async-start | bytes 2506752 | tf_op jit(solution)/shard_map/reduce_scatter | solution.py:198
  475.9 21.7 %all-to-all-start.6 = ((f32[16,2,2304]{2,1,0:T(2,128)}), f32[16,2,2304]{2,1,0:T(2,128)S(1)}, u32[]{:S(2)}, u32[]{:S(2)}) async-start(f32[16,2,2304]{2,1,0:T(2,128)} %reshape.385), calls=%async_computation.7 | async-start | bytes 589824 | tf_op jit(solution)/shard_map/all_to_all | solution.py:206
Sparse Core Ops, SparseCore 0:
  9.2 43.4 all-gather.3
  143.0 93.6 all-reduce.2
  269.4 48.1 all-gather.5
  399.7 74.3 reduce-scatter.1
